TPU v7x, 32 devices: a whole 2x2x4 slice. The times are simulated.
32 devices in a mesh: seq: 8 (over y, x, core), head: 4 (over z).
Axes of the slice: x: 2, y: 2, z: 4, core: 2. Of those that a mesh axis runs over, the one named last changes fastest.
Arguments:
- query_lin: bfloat16 [512, 4096], P('seq', 'head'), may hold values from -6 to 6
- key_lin: bfloat16 [512, 4096], P('seq', 'head'), may hold values from -6 to 6
- value_lin: bfloat16 [512, 4096], P('seq', 'head'), may hold values from -6 to 6
- log_decay: float32 [32, 512], P('head', 'seq'), may hold values from -1.6 to 0
- query_soft: bfloat16 [512, 4096], P(('seq', 'head')), may hold values from -4.5 to 4.5
- key_soft: bfloat16 [512, 512], P(('seq', 'head')), may hold values from -4.5 to 4.5
- value_soft: bfloat16 [512, 512], P(('seq', 'head')), may hold values from -6 to 6
- doc_start: int32 [512], P('seq'), may hold values from 0 to 480, as said below
Outputs:
- lin_out: bfloat16 [512, 4096], P('seq', 'head')
- soft_out: bfloat16 [512, 4096], P('seq', 'head')
- soft_lse: float32 [32, 512], P('head', 'seq')
Inputs may be any that keep to these rules, and one draw needn't show every extreme that they name: doc_start[t] is the first position of the document that holds token t: 0 for the first document, never above t, the same over a document; at most 4 documents; every document but the first and the last starts at a position of 1 to 32; the last document starts at 480.
All inputs are finite; a program needn't handle non-finite values.
Results may differ from a plain program's by a relative error of at most 0.003.
Values may be sent and summed in bfloat16 or wider, within the bound.
A program may use at most 256 MiB of HBM per device.

v0:
```python
import jax
import jax.numpy as jnp
from jax import lax
from jax.sharding import PartitionSpec as P

DH = 128
HIGHEST = lax.Precision.HIGHEST
masked_score = -1e30


def prefix(array, axis, combine, identity):
    size, here = (lax.axis_size(axis), lax.axis_index(axis))
    everything = jax.tree.map(lambda part: lax.all_gather(part, axis), array)
    start = jax.tree.map(
        lambda part, zero: jnp.broadcast_to(jnp.asarray(zero, part.dtype), part.shape),
        array,
        identity,
    )

    def lap(k, before):
        reached = k < here
        new = combine(before, jax.tree.map(lambda part: part[k], everything))
        return jax.tree.map(lambda a, b: jnp.where(reached, a, b), new, before)

    return lax.fori_loop(0, size, lap, start)


def span_terms(query_heads, key_heads, value_heads, decay_rows, doc_rows, first_place):
    span_len = query_heads.shape[0]
    cumulative = jnp.cumsum(decay_rows, axis=1)
    totals = cumulative[:, -1]
    token_positions = first_place + jnp.arange(span_len, dtype=jnp.int32)
    allowed = (token_positions[None, :] <= token_positions[:, None]) & (
        doc_rows[:, None] <= token_positions[None, :]
    )
    decay_gap = jnp.where(allowed[None], cumulative[:, :, None] - cumulative[:, None, :], 0.0)
    decay_mat = jnp.where(allowed[None], jnp.exp(decay_gap), 0.0)
    scores = jnp.einsum("thd,shd->hts", query_heads, key_heads, preferred_element_type=jnp.float32)
    key_float = key_heads.astype(jnp.float32)
    value_float = value_heads.astype(jnp.float32)
    inner_part = jnp.einsum("hts,shd->thd", scores * decay_mat, value_float, precision=HIGHEST)
    keep_mask = (doc_rows == doc_rows[-1]).astype(jnp.float32)
    tail_weight = jnp.exp(totals[:, None] - cumulative) * keep_mask[None, :]
    weighted_keys = key_float * jnp.transpose(tail_weight)[:, :, None]
    fresh_state = jnp.einsum("shd,she->hde", weighted_keys, value_float, precision=HIGHEST)
    carry_on = (doc_rows[-1] < first_place).astype(jnp.float32)
    factor = jnp.exp(totals) * carry_on
    read_mask = (doc_rows < first_place).astype(jnp.float32)[:, None] * jnp.transpose(
        jnp.exp(cumulative)
    )
    return (inner_part, fresh_state, factor, read_mask)


def combine_states(earlier, later_part):
    return (earlier[0] * later_part[0], later_part[0][:, None, None] * earlier[1] + later_part[1])


def lightning_part(query_lin, key_lin, value_lin, log_decay, doc_start):
    span_len = query_lin.shape[0]
    head_count = log_decay.shape[0]
    first_place = lax.axis_index("seq") * span_len
    query_heads = query_lin.reshape(span_len, head_count, DH)
    key_heads = key_lin.reshape(span_len, head_count, DH)
    value_heads = value_lin.reshape(span_len, head_count, DH)
    inner_part, fresh_state, factor, read_mask = span_terms(
        query_heads, key_heads, value_heads, log_decay, doc_start, first_place
    )
    identity = (jnp.ones((head_count,), jnp.float32), jnp.zeros((head_count, DH, DH), jnp.float32))
    unused, carried = prefix((factor, fresh_state), "seq", combine_states, identity)
    outer_part = (
        jnp.einsum("thd,hde->the", query_heads.astype(jnp.float32), carried, precision=HIGHEST)
        * read_mask[:, :, None]
    )
    mixed_out = inner_part + outer_part
    normed = mixed_out * lax.rsqrt(jnp.mean(mixed_out * mixed_out, axis=-1, keepdims=True) + 1e-06)
    return normed.astype(jnp.bfloat16).reshape(span_len, head_count * DH)


def softmax_part(query_soft, key_soft, value_soft, doc_start):
    queries, keys_local, values_local = (
        lax.all_to_all(query_soft, "head", split_axis=1, concat_axis=0, tiled=True),
        lax.all_to_all(key_soft, "head", split_axis=1, concat_axis=0, tiled=True),
        lax.all_to_all(value_soft, "head", split_axis=1, concat_axis=0, tiled=True),
    )
    span_len = queries.shape[0]
    kv_count = keys_local.shape[1] // DH
    group_size = queries.shape[1] // keys_local.shape[1]
    first_place = lax.axis_index("seq") * span_len
    query_places = first_place + jnp.arange(span_len, dtype=jnp.int32)
    query_heads = queries.reshape(span_len, kv_count, group_size, DH)
    score_scale = DH ** (-0.5)
    start_state = (
        jnp.full((span_len, kv_count, group_size), masked_score, jnp.float32),
        jnp.zeros((span_len, kv_count, group_size), jnp.float32),
        jnp.zeros((span_len, kv_count, group_size, DH), jnp.float32),
    )
    key_piece = lax.all_gather(keys_local, "seq", axis=0, tiled=True)
    value_piece = lax.all_gather(values_local, "seq", axis=0, tiled=True)
    piece_rows = key_piece.shape[0]
    block_rows = max(
        (divisor for divisor in range(1, min(piece_rows, 1024) + 1) if piece_rows % divisor == 0)
    )
    block_count = piece_rows // block_rows
    key_parts = key_piece.reshape(block_count, block_rows, kv_count, DH)
    value_parts = value_piece.reshape(block_count, block_rows, kv_count, DH)
    begin_rows = jnp.int32(0) + block_rows * jnp.arange(block_count, dtype=jnp.int32)

    def absorb_block(running, slices):
        key_block, value_block, begin_row = slices
        running_max, norm_sum, accum_out = running
        token_positions = begin_row + jnp.arange(block_rows, dtype=jnp.int32)
        allowed = (token_positions[None, :] <= query_places[:, None]) & (
            doc_start[:, None] <= token_positions[None, :]
        )
        allowed = allowed[:, None, None, :]
        scores = (
            jnp.einsum("tkgd,skd->tkgs", query_heads, key_block, preferred_element_type=jnp.float32)
            * score_scale
        )
        new_max = jnp.maximum(
            running_max, jnp.max(jnp.where(allowed, scores, masked_score), axis=-1)
        )
        raw_weight = jnp.where(allowed, jnp.exp(scores - new_max[..., None]), 0.0)
        shrink = jnp.exp(running_max - new_max)
        norm_sum = norm_sum * shrink + jnp.sum(raw_weight, axis=-1)
        accum_out = accum_out * shrink[..., None] + jnp.einsum(
            "tkgs,skd->tkgd",
            raw_weight.astype(jnp.bfloat16),
            value_block,
            preferred_element_type=jnp.float32,
        )
        running = (new_max, norm_sum, accum_out)
        return (running, None)

    final_state, unused = lax.scan(absorb_block, start_state, (key_parts, value_parts, begin_rows))
    running_max, norm_sum, accum_out = final_state
    soft_out = (
        (accum_out / norm_sum[..., None])
        .astype(jnp.bfloat16)
        .reshape(span_len, kv_count * group_size * DH)
    )
    soft_lse = jnp.transpose(
        (running_max + jnp.log(norm_sum)).reshape(span_len, kv_count * group_size)
    )
    return (soft_out, soft_lse)


def per_device(
    query_lin, key_lin, value_lin, log_decay, query_soft, key_soft, value_soft, doc_start
):
    lin_out = lightning_part(query_lin, key_lin, value_lin, log_decay, doc_start)
    soft_out, soft_lse = softmax_part(query_soft, key_soft, value_soft, doc_start)
    return (lin_out, soft_out, soft_lse)


def solution(mesh):
    return jax.shard_map(
        per_device,
        mesh=mesh,
        in_specs=(
            P("seq", "head"),
            P("seq", "head"),
            P("seq", "head"),
            P("head", "seq"),
            P(("seq", "head"), None),
            P(("seq", "head"), None),
            P(("seq", "head"), None),
            P("seq"),
        ),
        out_specs=(P("seq", "head"), P("seq", "head"), P("head", "seq")),
        check_vma=False,
    )
```

profile of v0, /device:TPU:0, one launch (start us, length us, event | category | flops | bytes accessed | tf_op | source)
XLA Modules:
  0.0 91.8 jit_solution(14963114871208304785)
XLA Ops:
  7.2 0.0 copy-start
  7.2 0.0 all-gather.4.cloned.1.call-start
  7.2 1.2 %slice.8 = s32[1]{0:T(128)} slice(s32[64]{0:T(128)} %param.17), slice={[63:64]} | slice | bytes 8 | tf_op jit(solution)/shard_map/slice | solution.py:46
  9.1 1.3 %compare_convert_fusion = (f32[64]{0:T(128)S(1)}, f32[64]{0:T(128)S(1)}) fusion(s32[64]{0:T(128)} %param.17, s32[]{:T(128)S(6)} %mul.138, s32[]{:T(128)} %bitcast.1), kind=kLoop, calls=%fused_computation.64 | loop fusion | flops 256 | bytes 776 | tf_op jit(solution)/shard_map/convert_element_type | solution.py:48
  10.4 0.9 reduce_window_sum.11
  11.3 0.2 slice_reduce_fusion
  11.5 0.1 multiply_bitcast_fusion
  11.6 2.4 %fusion.11 = f32[8,128,128]{2,1,0:T(8,128)} fusion(f32[64,8]{0,1:T(8,128)S(1)} %get-tuple-element.160, bf16[64,1024]{1,0:T(8,128)(2,1)S(1)} %copy-done, bf16[64,1024]{1,0:T(8,128)(2,1)} %param.11), kind=kOutput, calls=%fused_computation.22 | convolution fusion | flops 100794368 | bytes 788480 | tf_op jit(solution)/shard_map/shd,she->hde/dot_general | solution.py:45
  14.0 0.0 all-gather.4.cloned.1.call-update
  14.0 1.3 %copy_bitcast_fusion.4 = bf16[16,4,128]{2,0,1:T(8,128)(2,1)} fusion(bf16[16,512]{1,0:T(8,128)(2,1)} %param.15), kind=kLoop, calls=%fused_computation.50 | loop fusion | bytes 32768 | tf_op jit(solution)/shard_map/all_to_all | solution.py:82
  15.3 6.3 %all-to-all-start = ((bf16[16,4,128]{2,0,1:T(8,128)(2,1)}), bf16[16,4,128]{2,0,1:T(8,128)(2,1)S(1)}, u32[]{:S(2)}, u32[]{:S(2)}) async-start(bf16[16,4,128]{2,0,1:T(8,128)(2,1)} %copy_bitcast_fusion.4), calls=%async_computation | async-start | bytes 32768 | tf_op jit(solution)/shard_map/all_to_all | solution.py:82
  21.7 1.3 %copy_bitcast_fusion.3 = bf16[16,4,128]{2,0,1:T(8,128)(2,1)} fusion(bf16[16,512]{1,0:T(8,128)(2,1)} %param.16), kind=kLoop, calls=%fused_computation.49 | loop fusion | bytes 32768 | tf_op jit(solution)/shard_map/all_to_all | solution.py:83
  23.0 0.7 compare_and_fusion
  23.7 3.5 %all-to-all-done = bf16[16,4,128]{2,0,1:T(8,128)(2,1)S(1)} async-done(((bf16[16,4,128]{2,0,1:T(8,128)(2,1)}), bf16[16,4,128]{2,0,1:T(8,128)(2,1)S(1)}, u32[]{:S(2)}, u32[]{:S(2)}) %all-to-all-start) | async-done | bytes 16416 | tf_op jit(solution)/shard_map/all_to_all | solution.py:82
  27.3 3.3 %all-to-all-start.2 = ((bf16[16,4,128]{2,0,1:T(8,128)(2,1)}), bf16[16,4,128]{2,0,1:T(8,128)(2,1)S(1)}, u32[]{:S(2)}, u32[]{:S(2)}) async-start(bf16[16,4,128]{2,0,1:T(8,128)(2,1)} %copy_bitcast_fusion.3), calls=%async_computation.2 | async-start | bytes 32768 | tf_op jit(solution)/shard_map/all_to_all | solution.py:83
  30.5 1.2 %convolution_multiply_fusion.1 = f32[8,64,64]{2,1,0:T(8,128)S(1)} fusion(f32[8,64]{1,0:T(8,128)S(1)} %reduce_window_sum.11, pred[64,64]{1,0:T(8,128)(4,1)S(1)} %compare_and_fusion, bf16[64,1024]{1,0:T(8,128)(2,1)} %param.11, bf16[64,1024]{1,0:T(8,128)(2,1)} %param.10), kind=kOutput, calls=%fused_computation.10 | convolution fusion | flops 8519680 | bytes 399360 | tf_op jit(solution)/shard_map/thd,shd->hts/dot_general | solution.py:38
  31.7 1.2 %dynamic-slice = u32[1]{0:T(128)} dynamic-slice(u32[32]{0:T(128)} %constant.72, u32[]{:T(128)S(6)} %add.102), dynamic_slice_sizes={1} | dynamic-slice | bytes 12
  33.6 0.2 dynamic-update-slice
  33.9 12.5 %all-reduce = f32[64]{0:T(128)S(1)} all-reduce(f32[64]{0:T(128)S(1)} %dynamic-update-slice), channel_id=2, replica_groups=mesh['seq'=8,'head'=4] {'seq'}, use_global_device_ids=true, to_apply=%add | all-reduce | flops 64 | bytes 512
  46.4 0.1 reshape.236
  46.5 1.6 %copy.93 = bf16[2,4,8,1024]{3,2,0,1:T(8,128)(2,1)} copy(bf16[2,4,8,1024]{3,2,1,0:T(8,128)(2,1)} %bitcast.145) | data formatting | bytes 262144 | tf_op jit(solution)/shard_map/all_to_all | solution.py:81
  48.1 0.0 all-to-all-done.2
  48.1 4.8 %all-to-all-start.1 = ((bf16[16,4,1024]{2,0,1:T(8,128)(2,1)}), bf16[16,4,1024]{2,0,1:T(8,128)(2,1)S(1)}, u32[]{:S(2)}, u32[]{:S(2)}) async-start(bf16[16,4,1024]{2,0,1:T(8,128)(2,1)} %bitcast.137), calls=%async_computation.1 | async-start | bytes 262144 | tf_op jit(solution)/shard_map/all_to_all | solution.py:81
  52.8 0.7 fusion.25
  53.6 9.1 %all_gather.19 = bf16[512,128]{1,0:T(8,128)(2,1)S(1)} all-gather(bf16[64,128]{1,0:T(8,128)(2,1)S(1)} %bitcast.148), channel_id=1, replica_groups=mesh['seq'=8,'head'=4] {'seq'}, dimensions={0}, use_global_device_ids=true | all-gather | bytes 147456 | tf_op jit(solution)/shard_map/all_gather | solution.py:97
  62.7 8.4 %all_gather.20 = bf16[512,128]{1,0:T(8,128)(2,1)S(1)} all-gather(bf16[64,128]{1,0:T(8,128)(2,1)S(1)} %bitcast.149), channel_id=1, replica_groups=mesh['seq'=8,'head'=4] {'seq'}, dimensions={0}, use_global_device_ids=true | all-gather | bytes 147456 | tf_op jit(solution)/shard_map/all_gather | solution.py:98
  71.0 0.0 all-to-all-done.1
  71.1 0.4 select_reduce_fusion
  71.4 0.4 fusion.7
  71.8 0.1 copy.42
  71.9 0.1 copy.45
  72.0 0.5 fusion.6
  72.5 0.0 copy-start.1
  72.5 0.7 copy.92
  73.1 0.6 fusion.33
  73.8 9.7 %while.9 = (s32[]{:T(128)}, f32[8,128,128]{2,1,0:T(8,128)S(1)}, s32[]{:T(128)}, f32[8,8]{1,0:T(8,128)S(1)}, f32[8,8,128,128]{3,2,1,0:T(8,128)}, /*index=5*/s32[]{:T(128)}, s32[]{:T(128)}) while((s32[]{:T(128)}, f32[8,128,128]{2,1,0:T(8,128)S(1)}, s32[]{:T(128)}, f32[8,8]{1,0:T(8,128)S(1)}, f32[8,8,128,128]{3,2,1,0:T(8,128)}, ...), condition=%wide.region_2.3_spmd.clone, body=%wide.region_1.2_spmd.clone.sunk | while | flops 524292 | bytes 1573065 | solution.py:25
  73.8 1.2 %fusion.49 = f32[8,128,128]{2,1,0:T(8,128)S(1)} fusion(f32[8,8,128,128]{3,2,1,0:T(8,128)} %get-tuple-element.216, s32[]{:T(128)} %get-tuple-element.205, f32[8,128,128]{2,1,0:T(8,128)S(1)} %get-tuple-element.206, f32[8]{0:T(128)S(1)} %dynamic-slice_bitcast_fusion.2, pred[]{:T(512)S(6)} %compare.3, pred[]{:T(512)S(6)} %lt.33), kind=kLoop, calls=%fused_computation.1.clone.1 | loop fusion | flops 524288 | bytes 1572902 | tf_op jit(solution)/shard_map/while/body/eval_jaxpr/jit(_where)/select_n | solution.py:23
  75.0 1.2 %fusion.49 = f32[8,128,128]{2,1,0:T(8,128)S(1)} fusion(f32[8,8,128,128]{3,2,1,0:T(8,128)} %get-tuple-element.216, s32[]{:T(128)} %get-tuple-element.205, f32[8,128,128]{2,1,0:T(8,128)S(1)} %get-tuple-element.206, f32[8]{0:T(128)S(1)} %dynamic-slice_bitcast_fusion.2, pred[]{:T(512)S(6)} %compare.3, pred[]{:T(512)S(6)} %lt.33), kind=kLoop, calls=%fused_computation.1.clone.1 | loop fusion | flops 524288 | bytes 1572902 | tf_op jit(solution)/shard_map/while/body/eval_jaxpr/jit(_where)/select_n | solution.py:23
  76.2 1.2 %fusion.49 = f32[8,128,128]{2,1,0:T(8,128)S(1)} fusion(f32[8,8,128,128]{3,2,1,0:T(8,128)} %get-tuple-element.216, s32[]{:T(128)} %get-tuple-element.205, f32[8,128,128]{2,1,0:T(8,128)S(1)} %get-tuple-element.206, f32[8]{0:T(128)S(1)} %dynamic-slice_bitcast_fusion.2, pred[]{:T(512)S(6)} %compare.3, pred[]{:T(512)S(6)} %lt.33), kind=kLoop, calls=%fused_computation.1.clone.1 | loop fusion | flops 524288 | bytes 1572902 | tf_op jit(solution)/shard_map/while/body/eval_jaxpr/jit(_where)/select_n | solution.py:23
  77.4 1.2 %fusion.49 = f32[8,128,128]{2,1,0:T(8,128)S(1)} fusion(f32[8,8,128,128]{3,2,1,0:T(8,128)} %get-tuple-element.216, s32[]{:T(128)} %get-tuple-element.205, f32[8,128,128]{2,1,0:T(8,128)S(1)} %get-tuple-element.206, f32[8]{0:T(128)S(1)} %dynamic-slice_bitcast_fusion.2, pred[]{:T(512)S(6)} %compare.3, pred[]{:T(512)S(6)} %lt.33), kind=kLoop, calls=%fused_computation.1.clone.1 | loop fusion | flops 524288 | bytes 1572902 | tf_op jit(solution)/shard_map/while/body/eval_jaxpr/jit(_where)/select_n | solution.py:23
  78.6 1.2 %fusion.49 = f32[8,128,128]{2,1,0:T(8,128)S(1)} fusion(f32[8,8,128,128]{3,2,1,0:T(8,128)} %get-tuple-element.216, s32[]{:T(128)} %get-tuple-element.205, f32[8,128,128]{2,1,0:T(8,128)S(1)} %get-tuple-element.206, f32[8]{0:T(128)S(1)} %dynamic-slice_bitcast_fusion.2, pred[]{:T(512)S(6)} %compare.3, pred[]{:T(512)S(6)} %lt.33), kind=kLoop, calls=%fused_computation.1.clone.1 | loop fusion | flops 524288 | bytes 1572902 | tf_op jit(solution)/shard_map/while/body/eval_jaxpr/jit(_where)/select_n | solution.py:23
  79.8 1.2 %fusion.49 = f32[8,128,128]{2,1,0:T(8,128)S(1)} fusion(f32[8,8,128,128]{3,2,1,0:T(8,128)} %get-tuple-element.216, s32[]{:T(128)} %get-tuple-element.205, f32[8,128,128]{2,1,0:T(8,128)S(1)} %get-tuple-element.206, f32[8]{0:T(128)S(1)} %dynamic-slice_bitcast_fusion.2, pred[]{:T(512)S(6)} %compare.3, pred[]{:T(512)S(6)} %lt.33), kind=kLoop, calls=%fused_computation.1.clone.1 | loop fusion | flops 524288 | bytes 1572902 | tf_op jit(solution)/shard_map/while/body/eval_jaxpr/jit(_where)/select_n | solution.py:23
  81.0 1.2 %fusion.49 = f32[8,128,128]{2,1,0:T(8,128)S(1)} fusion(f32[8,8,128,128]{3,2,1,0:T(8,128)} %get-tuple-element.216, s32[]{:T(128)} %get-tuple-element.205, f32[8,128,128]{2,1,0:T(8,128)S(1)} %get-tuple-element.206, f32[8]{0:T(128)S(1)} %dynamic-slice_bitcast_fusion.2, pred[]{:T(512)S(6)} %compare.3, pred[]{:T(512)S(6)} %lt.33), kind=kLoop, calls=%fused_computation.1.clone.1 | loop fusion | flops 524288 | bytes 1572902 | tf_op jit(solution)/shard_map/while/body/eval_jaxpr/jit(_where)/select_n | solution.py:23
  82.2 1.2 %fusion.49 = f32[8,128,128]{2,1,0:T(8,128)S(1)} fusion(f32[8,8,128,128]{3,2,1,0:T(8,128)} %get-tuple-element.216, s32[]{:T(128)} %get-tuple-element.205, f32[8,128,128]{2,1,0:T(8,128)S(1)} %get-tuple-element.206, f32[8]{0:T(128)S(1)} %dynamic-slice_bitcast_fusion.2, pred[]{:T(512)S(6)} %compare.3, pred[]{:T(512)S(6)} %lt.33), kind=kLoop, calls=%fused_computation.1.clone.1 | loop fusion | flops 524288 | bytes 1572902 | tf_op jit(solution)/shard_map/while/body/eval_jaxpr/jit(_where)/select_n | solution.py:23
  83.4 0.0 copy-done.1
  83.4 0.4 fusion.2
  83.8 0.4 multiply_reduce_fusion
  84.2 0.8 copy_bitcast_fusion.1
  (17 shorter events, 0.1 us)
Async XLA Ops:
  7.2 4.4 %copy-start = (bf16[64,1024]{1,0:T(8,128)(2,1)S(1)}, bf16[64,1024]{1,0:T(8,128)(2,1)}, u32[]{:S(2)}) copy-start(bf16[64,1024]{1,0:T(8,128)(2,1)} %param.12) | copy-start | bytes 393220
  7.2 66.6 %all-gather.4.cloned.1.call-start = ((), (), s32[]{:S(2)}) async-start(), calls=%async_computation.3 | async-start | bytes 4718592 | tf_op jit(solution)/shard_map/all_gather | solution.py:13
  15.3 11.9 %all-to-all-start = ((bf16[16,4,128]{2,0,1:T(8,128)(2,1)}), bf16[16,4,128]{2,0,1:T(8,128)(2,1)S(1)}, u32[]{:S(2)}, u32[]{:S(2)}) async-start(bf16[16,4,128]{2,0,1:T(8,128)(2,1)} %copy_bitcast_fusion.4), calls=%async_computation | async-start | bytes 32768 | tf_op jit(solution)/shard_map/all_to_all | solution.py:82
  27.3 20.8 %all-to-all-start.2 = ((bf16[16,4,128]{2,0,1:T(8,128)(2,1)}), bf16[16,4,128]{2,0,1:T(8,128)(2,1)S(1)}, u32[]{:S(2)}, u32[]{:S(2)}) async-start(bf16[16,4,128]{2,0,1:T(8,128)(2,1)} %copy_bitcast_fusion.3), calls=%async_computation.2 | async-start | bytes 32768 | tf_op jit(solution)/shard_map/all_to_all | solution.py:83
  48.1 23.0 %all-to-all-start.1 = ((bf16[16,4,1024]{2,0,1:T(8,128)(2,1)}), bf16[16,4,1024]{2,0,1:T(8,128)(2,1)S(1)}, u32[]{:S(2)}, u32[]{:S(2)}) async-start(bf16[16,4,1024]{2,0,1:T(8,128)(2,1)} %bitcast.137), calls=%async_computation.1 | async-start | bytes 262144 | tf_op jit(solution)/shard_map/all_to_all | solution.py:81
  72.5 11.0 %copy-start.1 = (bf16[64,1024]{1,0:T(8,128)(2,1)S(1)}, bf16[64,1024]{1,0:T(8,128)(2,1)}, u32[]{:S(2)}) copy-start(bf16[64,1024]{1,0:T(8,128)(2,1)} %param.10) | copy-start | bytes 393220
Sparse Core Ops, SparseCore 0:
  14.1 39.5 all-gather.3
where the time goes:
time: 92.9 us; the launch traced here: 91.8 us
  blocking collectives  30 us (32%)
  between operations  15.5 us (17%)
  other arithmetic  15.1 us (16%)
  starting transfers between devices  14.4 us (16%)
  local copies, waits for them, and re-layouts  7.97 us (9%)
  matrix products  5.12 us (6%)
  waiting for transfers between devices  3.56 us (4%)
    unnamed x1, blocking collectives  12.5 us
    select_n x8, other arithmetic, lap(): return jax.tree.map(lambda a, b: jnp.where(reached, a, b), new, before)  9.38 us
    all_gather x1, blocking collectives, softmax_part(): key_piece = lax.all_gather(keys_local, 'seq', axis=0, tiled=True)  9.07 us
    all_gather x1, blocking collectives, softmax_part(): value_piece = lax.all_gather(values_local, 'seq', axis=0, tiled=True)  8.36 us
    all_to_all x1, starting transfers between devices, softmax_part(): lax.all_to_all(key_soft, 'head', split_axis=1, concat_axis=0, tiled=True)  6.32 us
    all_to_all x1, starting transfers between devices, softmax_part(): lax.all_to_all(query_soft, 'head', split_axis=1, concat_axis=0, tiled=True)  4.78 us
    all_to_all x1, waiting for transfers between devices, softmax_part(): lax.all_to_all(key_soft, 'head', split_axis=1, concat_axis=0, tiled=True)  3.54 us
    all_to_all x1, starting transfers between devices, softmax_part(): lax.all_to_all(value_soft, 'head', split_axis=1, concat_axis=0, tiled=True)  3.25 us
  transfers between devices with their start and end apart: 4, of which 1 were waited for; matrix products, arithmetic and copies ran while one was open for 12% of the time, Pallas kernels for 0%

commit v1 on v0

--- a/solution.py
+++ b/solution.py
@@ -94,7 +94,16 @@
         jnp.zeros((span_len, kv_count, group_size), jnp.float32),
         jnp.zeros((span_len, kv_count, group_size, DH), jnp.float32),
     )
-    key_piece = lax.all_gather(keys_local, "seq", axis=0, tiled=True)
+    axis_n = lax.psum(1, axis_name="seq")
+    buffer = [(dev, (dev + 1) % axis_n) for dev in range(axis_n)]
+    z1 = [None] * axis_n
+    z1[axis_n - 1] = keys_local
+    for dd in range(axis_n - 2, -1, -1):
+        z1[dd] = lax.ppermute(z1[dd + 1], axis_name="seq", perm=buffer)
+    x_next = jnp.concatenate(z1, axis=0)
+    long_array = lax.axis_index("seq")
+    a_next = (long_array + 1) * keys_local.shape[0]
+    key_piece = jnp.roll(x_next, shift=a_next, axis=0)
     value_piece = lax.all_gather(values_local, "seq", axis=0, tiled=True)
     piece_rows = key_piece.shape[0]
     block_rows = max(

time: 92.9 us -> 104 us (1.12)
  waiting for transfers between devices: 3.56 us -> 14.6 us
  blocking collectives: 30 us -> 35.4 us
  starting transfers between devices: 14.4 us -> 9.12 us
    ppermute x0 -> x7, waiting for transfers between devices: none -> 14.5 us  [softmax_part(): z1[dd] = lax.ppermute(z1[dd + 1], axis_name='seq', perm=buffer)]
    all_to_all x0 -> x1, blocking collectives: none -> 11.7 us  [softmax_part(): lax.all_to_all(key_soft, 'head', split_axis=1, concat_axis=0, tiled=True)]
    all_gather x1 -> x0, blocking collectives: 9.07 us -> none  [softmax_part(): key_piece = lax.all_gather(keys_local, 'seq', axis=0, tiled=True)]
    all_to_all x1 -> x0, starting transfers between devices: 6.32 us -> none  [softmax_part(): lax.all_to_all(key_soft, 'head', split_axis=1, concat_axis=0, tiled=True)]
    all_to_all x1 -> x0, waiting for transfers between devices: 3.54 us -> none  [softmax_part(): lax.all_to_all(key_soft, 'head', split_axis=1, concat_axis=0, tiled=True)]
    unnamed x1, blocking collectives: 12.5 us -> 14.4 us
    unnamed x9 -> x24, local copies, waits for them, and re-layouts: 2.2 us -> 2.33 us
  transfers between devices with their start and end apart: 4 -> 10, of which waited for: 1 -> 4; matrix products, arithmetic and copies ran while one was open for 12% -> 10% of each run, Pallas kernels for 0% -> 0%
where the time goes in v1:
time: 104 us; the launch traced here: 103 us
  blocking collectives  35.4 us (34%)
  between operations  15.6 us (15%)
  other arithmetic  15.1 us (15%)
  waiting for transfers between devices  14.6 us (14%)
  starting transfers between devices  9.12 us (9%)
  local copies, waits for them, and re-layouts  7.51 us (7%)
  matrix products  5.14 us (5%)
    ppermute x7, waiting for transfers between devices, softmax_part(): z1[dd] = lax.ppermute(z1[dd + 1], axis_name='seq', perm=buffer)  14.5 us
    unnamed x1, blocking collectives  14.4 us
    all_to_all x1, blocking collectives, softmax_part(): lax.all_to_all(key_soft, 'head', split_axis=1, concat_axis=0, tiled=True)  11.7 us
    select_n x8, other arithmetic, lap(): return jax.tree.map(lambda a, b: jnp.where(reached, a, b), new, before)  9.38 us
    all_gather x1, blocking collectives, softmax_part(): value_piece = lax.all_gather(values_local, 'seq', axis=0, tiled=True)  9.32 us
    all_to_all x1, starting transfers between devices, softmax_part(): lax.all_to_all(query_soft, 'head', split_axis=1, concat_axis=0, tiled=True)  5.06 us
    all_to_all x1, starting transfers between devices, softmax_part(): lax.all_to_all(value_soft, 'head', split_axis=1, concat_axis=0, tiled=True)  3.25 us
    dot_general x1, matrix products, span_terms(): jnp.einsum('shd,she->hde', weighted_keys, value_float, precision=HIGHEST)  2.4 us
  transfers between devices with their start and end apart: 10, of which 4 were waited for; matrix products, arithmetic and copies ran while one was open for 10% of the time, Pallas kernels for 0%

profile of v1, /device:TPU:0, one launch (start us, length us, event | category | flops | bytes accessed | tf_op | source)
XLA Modules:
  0.0 102.7 jit_solution(15270654322910318573)
XLA Ops:
  7.2 0.0 copy-start
  7.2 0.0 all-gather.4.cloned.1.call-start
  7.2 1.2 %slice.8 = s32[1]{0:T(128)} slice(s32[64]{0:T(128)} %param.17), slice={[63:64]} | slice | bytes 8 | tf_op jit(solution)/shard_map/slice | solution.py:46
  9.1 1.3 %compare_convert_fusion = (f32[64]{0:T(128)S(1)}, f32[64]{0:T(128)S(1)}) fusion(s32[64]{0:T(128)} %param.17, s32[]{:T(128)S(6)} %mul.141, s32[]{:T(128)} %bitcast.1), kind=kLoop, calls=%fused_computation.81 | loop fusion | flops 256 | bytes 776 | tf_op jit(solution)/shard_map/convert_element_type | solution.py:48
  10.4 0.9 reduce_window_sum.11
  11.3 0.2 slice_reduce_fusion
  11.5 0.1 multiply_bitcast_fusion
  11.6 2.4 %fusion.11 = f32[8,128,128]{2,1,0:T(8,128)} fusion(f32[64,8]{0,1:T(8,128)S(1)} %get-tuple-element.160, bf16[64,1024]{1,0:T(8,128)(2,1)S(1)} %copy-done, bf16[64,1024]{1,0:T(8,128)(2,1)} %param.11), kind=kOutput, calls=%fused_computation.22 | convolution fusion | flops 100794368 | bytes 788480 | tf_op jit(solution)/shard_map/shd,she->hde/dot_general | solution.py:45
  14.0 0.0 all-gather.4.cloned.1.call-update
  14.0 0.7 copy_bitcast_fusion.4
  14.7 11.7 %all_to_all.54 = bf16[16,4,128]{2,0,1:T(8,128)(2,1)S(1)} all-to-all(bf16[16,4,128]{2,0,1:T(8,128)(2,1)S(1)} %copy_bitcast_fusion.4), channel_id=1, replica_groups=mesh['seq'=8,'head'=4] {'head'}, dimensions={1} | all-to-all | bytes 32768 | tf_op jit(solution)/shard_map/all_to_all | solution.py:82
  26.5 4.4 %collective-permute-done = bf16[64,128]{1,0:T(8,128)(2,1)S(1)} collective-permute-done((bf16[64,128]{1,0:T(8,128)(2,1)S(1)}, bf16[64,128]{1,0:T(8,128)(2,1)S(1)}, u32[]{:S(2)}, u32[]{:S(2)}) %collective-permute-start) | collective-permute-done | bytes 16416 | tf_op jit(solution)/shard_map/ppermute | solution.py:102
  30.9 1.3 %copy_bitcast_fusion.3 = bf16[16,4,128]{2,0,1:T(8,128)(2,1)} fusion(bf16[16,512]{1,0:T(8,128)(2,1)} %param.16), kind=kLoop, calls=%fused_computation.66 | loop fusion | bytes 32768 | tf_op jit(solution)/shard_map/all_to_all | solution.py:83
  32.2 3.3 %all-to-all-start.2 = ((bf16[16,4,128]{2,0,1:T(8,128)(2,1)}), bf16[16,4,128]{2,0,1:T(8,128)(2,1)S(1)}, u32[]{:S(2)}, u32[]{:S(2)}) async-start(bf16[16,4,128]{2,0,1:T(8,128)(2,1)} %copy_bitcast_fusion.3), calls=%async_computation.2 | async-start | bytes 32768 | tf_op jit(solution)/shard_map/all_to_all | solution.py:83
  35.4 0.8 collective-permute-start.2
  36.2 3.4 %collective-permute-done.2 = bf16[64,128]{1,0:T(8,128)(2,1)S(1)} collective-permute-done((bf16[64,128]{1,0:T(8,128)(2,1)S(1)}, bf16[64,128]{1,0:T(8,128)(2,1)S(1)}, u32[]{:S(2)}, u32[]{:S(2)}) %collective-permute-start.2) | collective-permute-done | bytes 16416 | tf_op jit(solution)/shard_map/ppermute | solution.py:102
  39.6 0.7 compare_and_fusion
  40.3 3.6 %collective-permute-done.3 = bf16[64,128]{1,0:T(8,128)(2,1)S(1)} collective-permute-done((bf16[64,128]{1,0:T(8,128)(2,1)S(1)}, bf16[64,128]{1,0:T(8,128)(2,1)S(1)}, u32[]{:S(2)}, u32[]{:S(2)}) %collective-permute-start.3) | collective-permute-done | bytes 16416 | tf_op jit(solution)/shard_map/ppermute | solution.py:102
  43.9 1.2 %convolution_multiply_fusion.1 = f32[8,64,64]{2,1,0:T(8,128)S(1)} fusion(f32[8,64]{1,0:T(8,128)S(1)} %reduce_window_sum.11, pred[64,64]{1,0:T(8,128)(4,1)S(1)} %compare_and_fusion, bf16[64,1024]{1,0:T(8,128)(2,1)} %param.11, bf16[64,1024]{1,0:T(8,128)(2,1)} %param.10), kind=kOutput, calls=%fused_computation.10 | convolution fusion | flops 8519680 | bytes 399360 | tf_op jit(solution)/shard_map/thd,shd->hts/dot_general | solution.py:38
  45.1 3.2 %collective-permute-done.4 = bf16[64,128]{1,0:T(8,128)(2,1)S(1)} collective-permute-done((bf16[64,128]{1,0:T(8,128)(2,1)S(1)}, bf16[64,128]{1,0:T(8,128)(2,1)S(1)}, u32[]{:S(2)}, u32[]{:S(2)}) %collective-permute-start.4) | collective-permute-done | bytes 16416 | tf_op jit(solution)/shard_map/ppermute | solution.py:102
  48.3 0.7 fusion.26
  49.1 1.2 %dynamic-slice = u32[1]{0:T(128)} dynamic-slice(u32[32]{0:T(128)} %constant.95, u32[]{:T(128)S(6)} %add.118), dynamic_slice_sizes={1} | dynamic-slice | bytes 12
  51.0 0.2 dynamic-update-slice
  51.2 14.4 %all-reduce = f32[64]{0:T(128)S(1)} all-reduce(f32[64]{0:T(128)S(1)} %dynamic-update-slice), channel_id=2, replica_groups=mesh['seq'=8,'head'=4] {'seq'}, use_global_device_ids=true, to_apply=%add | all-reduce | flops 64 | bytes 512
  65.6 0.1 reshape.236
  65.7 1.6 %copy.93 = bf16[2,4,8,1024]{3,2,0,1:T(8,128)(2,1)} copy(bf16[2,4,8,1024]{3,2,1,0:T(8,128)(2,1)} %bitcast.148) | data formatting | bytes 262144 | tf_op jit(solution)/shard_map/all_to_all | solution.py:81
  67.3 5.1 %all-to-all-start.1 = ((bf16[16,4,1024]{2,0,1:T(8,128)(2,1)}), bf16[16,4,1024]{2,0,1:T(8,128)(2,1)S(1)}, u32[]{:S(2)}, u32[]{:S(2)}) async-start(bf16[16,4,1024]{2,0,1:T(8,128)(2,1)} %bitcast.137), calls=%async_computation.1 | async-start | bytes 262144 | tf_op jit(solution)/shard_map/all_to_all | solution.py:81
  72.4 9.3 %all_gather.16 = bf16[512,128]{1,0:T(8,128)(2,1)S(1)} all-gather(bf16[64,128]{1,0:T(8,128)(2,1)S(1)} %bitcast.151), channel_id=1, replica_groups=mesh['seq'=8,'head'=4] {'seq'}, dimensions={0}, use_global_device_ids=true | all-gather | bytes 147456 | tf_op jit(solution)/shard_map/all_gather | solution.py:107
  81.9 0.4 select_reduce_fusion
  82.3 0.4 fusion.7
  82.7 0.1 copy.45
  82.8 0.1 copy.42
  82.9 0.4 fusion.6
  83.3 0.0 copy-start.1
  83.3 0.7 copy.92
  84.0 0.6 fusion.34
  84.6 9.7 %while.9 = (s32[]{:T(128)}, f32[8,128,128]{2,1,0:T(8,128)S(1)}, s32[]{:T(128)}, f32[8,8]{1,0:T(8,128)S(1)}, f32[8,8,128,128]{3,2,1,0:T(8,128)}, /*index=5*/s32[]{:T(128)}, s32[]{:T(128)}) while((s32[]{:T(128)}, f32[8,128,128]{2,1,0:T(8,128)S(1)}, s32[]{:T(128)}, f32[8,8]{1,0:T(8,128)S(1)}, f32[8,8,128,128]{3,2,1,0:T(8,128)}, ...), condition=%wide.region_2.3_spmd.clone, body=%wide.region_1.2_spmd.clone.sunk | while | flops 524292 | bytes 1573073 | solution.py:25
  84.6 1.2 %fusion.51 = f32[8,128,128]{2,1,0:T(8,128)S(1)} fusion(f32[8,8,128,128]{3,2,1,0:T(8,128)} %get-tuple-element.216, s32[]{:T(128)S(6)} %copy.97, f32[8,128,128]{2,1,0:T(8,128)S(1)} %get-tuple-element.206, f32[8]{0:T(128)S(1)} %dynamic-slice_bitcast_fusion.2, pred[]{:T(512)S(6)} %compare.4, pred[]{:T(512)S(6)} %lt.47), kind=kLoop, calls=%fused_computation.1.clone.1 | loop fusion | flops 524288 | bytes 1572902 | tf_op jit(solution)/shard_map/while/body/eval_jaxpr/jit(_where)/select_n | solution.py:23
  85.8 1.2 %fusion.51 = f32[8,128,128]{2,1,0:T(8,128)S(1)} fusion(f32[8,8,128,128]{3,2,1,0:T(8,128)} %get-tuple-element.216, s32[]{:T(128)S(6)} %copy.97, f32[8,128,128]{2,1,0:T(8,128)S(1)} %get-tuple-element.206, f32[8]{0:T(128)S(1)} %dynamic-slice_bitcast_fusion.2, pred[]{:T(512)S(6)} %compare.4, pred[]{:T(512)S(6)} %lt.47), kind=kLoop, calls=%fused_computation.1.clone.1 | loop fusion | flops 524288 | bytes 1572902 | tf_op jit(solution)/shard_map/while/body/eval_jaxpr/jit(_where)/select_n | solution.py:23
  87.1 1.2 %fusion.51 = f32[8,128,128]{2,1,0:T(8,128)S(1)} fusion(f32[8,8,128,128]{3,2,1,0:T(8,128)} %get-tuple-element.216, s32[]{:T(128)S(6)} %copy.97, f32[8,128,128]{2,1,0:T(8,128)S(1)} %get-tuple-element.206, f32[8]{0:T(128)S(1)} %dynamic-slice_bitcast_fusion.2, pred[]{:T(512)S(6)} %compare.4, pred[]{:T(512)S(6)} %lt.47), kind=kLoop, calls=%fused_computation.1.clone.1 | loop fusion | flops 524288 | bytes 1572902 | tf_op jit(solution)/shard_map/while/body/eval_jaxpr/jit(_where)/select_n | solution.py:23
  88.3 1.2 %fusion.51 = f32[8,128,128]{2,1,0:T(8,128)S(1)} fusion(f32[8,8,128,128]{3,2,1,0:T(8,128)} %get-tuple-element.216, s32[]{:T(128)S(6)} %copy.97, f32[8,128,128]{2,1,0:T(8,128)S(1)} %get-tuple-element.206, f32[8]{0:T(128)S(1)} %dynamic-slice_bitcast_fusion.2, pred[]{:T(512)S(6)} %compare.4, pred[]{:T(512)S(6)} %lt.47), kind=kLoop, calls=%fused_computation.1.clone.1 | loop fusion | flops 524288 | bytes 1572902 | tf_op jit(solution)/shard_map/while/body/eval_jaxpr/jit(_where)/select_n | solution.py:23
  89.5 1.2 %fusion.51 = f32[8,128,128]{2,1,0:T(8,128)S(1)} fusion(f32[8,8,128,128]{3,2,1,0:T(8,128)} %get-tuple-element.216, s32[]{:T(128)S(6)} %copy.97, f32[8,128,128]{2,1,0:T(8,128)S(1)} %get-tuple-element.206, f32[8]{0:T(128)S(1)} %dynamic-slice_bitcast_fusion.2, pred[]{:T(512)S(6)} %compare.4, pred[]{:T(512)S(6)} %lt.47), kind=kLoop, calls=%fused_computation.1.clone.1 | loop fusion | flops 524288 | bytes 1572902 | tf_op jit(solution)/shard_map/while/body/eval_jaxpr/jit(_where)/select_n | solution.py:23
  90.7 1.2 %fusion.51 = f32[8,128,128]{2,1,0:T(8,128)S(1)} fusion(f32[8,8,128,128]{3,2,1,0:T(8,128)} %get-tuple-element.216, s32[]{:T(128)S(6)} %copy.97, f32[8,128,128]{2,1,0:T(8,128)S(1)} %get-tuple-element.206, f32[8]{0:T(128)S(1)} %dynamic-slice_bitcast_fusion.2, pred[]{:T(512)S(6)} %compare.4, pred[]{:T(512)S(6)} %lt.47), kind=kLoop, calls=%fused_computation.1.clone.1 | loop fusion | flops 524288 | bytes 1572902 | tf_op jit(solution)/shard_map/while/body/eval_jaxpr/jit(_where)/select_n | solution.py:23
  91.9 1.2 %fusion.51 = f32[8,128,128]{2,1,0:T(8,128)S(1)} fusion(f32[8,8,128,128]{3,2,1,0:T(8,128)} %get-tuple-element.216, s32[]{:T(128)S(6)} %copy.97, f32[8,128,128]{2,1,0:T(8,128)S(1)} %get-tuple-element.206, f32[8]{0:T(128)S(1)} %dynamic-slice_bitcast_fusion.2, pred[]{:T(512)S(6)} %compare.4, pred[]{:T(512)S(6)} %lt.47), kind=kLoop, calls=%fused_computation.1.clone.1 | loop fusion | flops 524288 | bytes 1572902 | tf_op jit(solution)/shard_map/while/body/eval_jaxpr/jit(_where)/select_n | solution.py:23
  93.1 1.2 %fusion.51 = f32[8,128,128]{2,1,0:T(8,128)S(1)} fusion(f32[8,8,128,128]{3,2,1,0:T(8,128)} %get-tuple-element.216, s32[]{:T(128)S(6)} %copy.97, f32[8,128,128]{2,1,0:T(8,128)S(1)} %get-tuple-element.206, f32[8]{0:T(128)S(1)} %dynamic-slice_bitcast_fusion.2, pred[]{:T(512)S(6)} %compare.4, pred[]{:T(512)S(6)} %lt.47), kind=kLoop, calls=%fused_computation.1.clone.1 | loop fusion | flops 524288 | bytes 1572902 | tf_op jit(solution)/shard_map/while/body/eval_jaxpr/jit(_where)/select_n | solution.py:23
  94.3 0.4 fusion.2
  94.7 0.4 multiply_reduce_fusion
  95.1 0.8 copy_bitcast_fusion.1
  (45 shorter events, 0.3 us)
Async XLA Ops:
  7.2 4.4 %copy-start = (bf16[64,1024]{1,0:T(8,128)(2,1)S(1)}, bf16[64,1024]{1,0:T(8,128)(2,1)}, u32[]{:S(2)}) copy-start(bf16[64,1024]{1,0:T(8,128)(2,1)} %param.12) | copy-start | bytes 393220
  7.2 77.4 %all-gather.4.cloned.1.call-start = ((), (), s32[]{:S(2)}) async-start(), calls=%async_computation.3 | async-start | bytes 4718592 | tf_op jit(solution)/shard_map/all_gather | solution.py:13
  26.5 4.4 %collective-permute-start = (bf16[64,128]{1,0:T(8,128)(2,1)S(1)}, bf16[64,128]{1,0:T(8,128)(2,1)S(1)}, u32[]{:S(2)}, u32[]{:S(2)}) collective-permute-start(bf16[64,128]{1,0:T(8,128)(2,1)S(1)} %bitcast.145), channel_id=1, source_target_pairs={{0,4},{4,8},{8,12},{12,16},{16,20},{20,24},{24,28},{28,0},{1,5},{5... | collective-permute-start | bytes 49160 | tf_op jit(solution)/shard_map/ppermute | solution.py:102
  30.8 4.6 %collective-permute-start.1 = (bf16[64,128]{1,0:T(8,128)(2,1)S(1)}, bf16[64,128]{1,0:T(8,128)(2,1)S(1)}, u32[]{:S(2)}, u32[]{:S(2)}) collective-permute-start(bf16[64,128]{1,0:T(8,128)(2,1)S(1)} %collective-permute-done), channel_id=1, source_target_pairs={{0,4},{4,8},{8,12},{12,16},{16,20},{20,24},{24,28},{28,0},{1,5},{5... | collective-permute-start | bytes 49160 | tf_op jit(solution)/shard_map/ppermute | solution.py:102
  32.2 35.1 %all-to-all-start.2 = ((bf16[16,4,128]{2,0,1:T(8,128)(2,1)}), bf16[16,4,128]{2,0,1:T(8,128)(2,1)S(1)}, u32[]{:S(2)}, u32[]{:S(2)}) async-start(bf16[16,4,128]{2,0,1:T(8,128)(2,1)} %copy_bitcast_fusion.3), calls=%async_computation.2 | async-start | bytes 32768 | tf_op jit(solution)/shard_map/all_to_all | solution.py:83
  35.4 4.1 %collective-permute-start.2 = (bf16[64,128]{1,0:T(8,128)(2,1)S(1)}, bf16[64,128]{1,0:T(8,128)(2,1)S(1)}, u32[]{:S(2)}, u32[]{:S(2)}) collective-permute-start(bf16[64,128]{1,0:T(8,128)(2,1)S(1)} %collective-permute-done.1), channel_id=1, source_target_pairs={{0,4},{4,8},{8,12},{12,16},{16,20},{20,24},{24,28},{28,0},{1,5},{5... | collective-permute-start | bytes 49160 | tf_op jit(solution)/shard_map/ppermute | solution.py:102
  39.6 4.3 %collective-permute-start.3 = (bf16[64,128]{1,0:T(8,128)(2,1)S(1)}, bf16[64,128]{1,0:T(8,128)(2,1)S(1)}, u32[]{:S(2)}, u32[]{:S(2)}) collective-permute-start(bf16[64,128]{1,0:T(8,128)(2,1)S(1)} %collective-permute-done.2), channel_id=1, source_target_pairs={{0,4},{4,8},{8,12},{12,16},{16,20},{20,24},{24,28},{28,0},{1,5},{5... | collective-permute-start | bytes 49160 | tf_op jit(solution)/shard_map/ppermute | solution.py:102
  43.9 4.4 %collective-permute-start.4 = (bf16[64,128]{1,0:T(8,128)(2,1)S(1)}, bf16[64,128]{1,0:T(8,128)(2,1)S(1)}, u32[]{:S(2)}, u32[]{:S(2)}) collective-permute-start(bf16[64,128]{1,0:T(8,128)(2,1)S(1)} %collective-permute-done.3), channel_id=1, source_target_pairs={{0,4},{4,8},{8,12},{12,16},{16,20},{20,24},{24,28},{28,0},{1,5},{5... | collective-permute-start | bytes 49160 | tf_op jit(solution)/shard_map/ppermute | solution.py:102
  48.3 19.0 %collective-permute-start.5 = (bf16[64,128]{1,0:T(8,128)(2,1)S(1)}, bf16[64,128]{1,0:T(8,128)(2,1)S(1)}, u32[]{:S(2)}, u32[]{:S(2)}) collective-permute-start(bf16[64,128]{1,0:T(8,128)(2,1)S(1)} %collective-permute-done.4), channel_id=1, source_target_pairs={{0,4},{4,8},{8,12},{12,16},{16,20},{20,24},{24,28},{28,0},{1,5},{5... | collective-permute-start | bytes 49160 | tf_op jit(solution)/shard_map/ppermute | solution.py:102
  67.3 14.4 %collective-permute-start.6 = (bf16[64,128]{1,0:T(8,128)(2,1)S(1)}, bf16[64,128]{1,0:T(8,128)(2,1)S(1)}, u32[]{:S(2)}, u32[]{:S(2)}) collective-permute-start(bf16[64,128]{1,0:T(8,128)(2,1)S(1)} %collective-permute-done.5), channel_id=1, source_target_pairs={{0,4},{4,8},{8,12},{12,16},{16,20},{20,24},{24,28},{28,0},{1,5},{5... | collective-permute-start | bytes 49160 | tf_op jit(solution)/shard_map/ppermute | solution.py:102
  67.3 14.6 %all-to-all-start.1 = ((bf16[16,4,1024]{2,0,1:T(8,128)(2,1)}), bf16[16,4,1024]{2,0,1:T(8,128)(2,1)S(1)}, u32[]{:S(2)}, u32[]{:S(2)}) async-start(bf16[16,4,1024]{2,0,1:T(8,128)(2,1)} %bitcast.137), calls=%async_computation.1 | async-start | bytes 262144 | tf_op jit(solution)/shard_map/all_to_all | solution.py:81
  83.3 11.0 %copy-start.1 = (bf16[64,1024]{1,0:T(8,128)(2,1)S(1)}, bf16[64,1024]{1,0:T(8,128)(2,1)}, u32[]{:S(2)}) copy-start(bf16[64,1024]{1,0:T(8,128)(2,1)} %param.10) | copy-start | bytes 393220
Sparse Core Ops, SparseCore 0:
  14.1 39.9 all-gather.3
